TPU v7x, 128 devices: a whole 4x4x4 slice. The times are simulated.
128 devices in a mesh: row: 8 (over x, core), col: 16 (over z, y).
Axes of the slice: x: 4, y: 4, z: 4, core: 2. Of those that a mesh axis runs over, the one named last changes fastest.
Arguments:
- features: bfloat16 [32768, 256], P('row'), may hold values from -6 to 6
- join_weight: bfloat16 [256, 256], replicated, may hold values from -0.375 to 0.375
- partner: int32 [32768], replicated, may hold values from 0 to 32767, as said below
- tile_index: int32 [13312], P(('row', 'col')), may hold values from 0 to 127, as said below
- tile_values: bfloat16 [13312, 256, 256], P(('row', 'col')), may hold values from 0 to 10
- pert_slot: int32 [512], P(('row', 'col')), may hold values from 0 to 103
- pert_values: bfloat16 [512, 256, 256], P(('row', 'col')), may hold values from 0 to 0.5
- routes: int32 [13312, 2], P(('row', 'col')), may hold values from 0 to 127, as said below
Outputs:
- coarse_features: bfloat16 [16384, 256], P('row')
- coarse_quarters: bfloat16 [32768, 128, 128], P(('row', 'col'))
Inputs may be any that keep to these rules, and one draw needn't show every extreme that they name: `partner`: fine nodes 16384 + k * 256 + j and k * 256 + s are partners of each other, where s runs over a permutation of the 256 slots for each coarse tile k. `tile_index`: each entry is a local tile position i * 8 + j with i below 16; the entries of one device are distinct; the four devices whose row indices agree modulo 8 // 2 and whose col indices agree modulo 16 // 2 hold the same list in the same order. `routes`: every column of a row equals column 0. Among the 104 rows of one device no device number appears more than 2 times, and in every draw some device number appears exactly 2 times among one device's rows.
All inputs are finite; a program needn't handle non-finite values.
Results may differ from a plain program's by a relative error of at most 0.0052.
Values may be sent and summed in bfloat16 or wider, within the bound.
No kernel may reach another device: no remote copies, remote signals or barrier semaphores. Data moves between devices by JAX's collectives and lax.ppermute only.
A program may use at most 192 MiB of HBM per device.

v0:
```python
import jax
import jax.numpy as jnp
from jax import lax
from jax.sharding import PartitionSpec as P


def swapped(value, axis, stride):
    mask = 2**stride
    pairs = [(source, source ^ mask) for source in range(lax.axis_size(axis))]
    return lax.ppermute(value, axis, pairs)


def pairing_table(slot_table, table_width):
    levels = lax.broadcasted_iota(jnp.int32, slot_table.shape + (table_width,), slot_table.ndim)
    return (slot_table[..., None] == levels).astype(jnp.bfloat16)


def keep_block(tile_block):
    return tile_block


def local(features, join_weight, partner, tile_index, tile_values, pert_slot, pert_values, routes):
    row_count = lax.axis_size("row")
    col_count = lax.axis_size("col")
    row_half = row_count // 2
    col_half = col_count // 2
    row_bit = row_count.bit_length() - 2
    col_bit = col_count.bit_length() - 2
    row_index = lax.axis_index("row")
    col_index = lax.axis_index("col")
    row_side = row_index // row_half
    col_side = col_index // col_half
    tile_size = tile_values.shape[1]
    half_tile = tile_size // 2
    slot_count = tile_values.shape[0]
    feat_width = features.shape[1]
    tiles_row = features.shape[0] // tile_size
    node_count = partner.shape[0]
    tiles_col = node_count // tile_size // col_count
    coarse_count = node_count // tile_size // 2
    coarse_nodes = coarse_count * tile_size
    capacity = routes.shape[1]
    receive_slots = row_count * col_count * capacity
    row_start = row_index % row_half * tiles_row
    col_start = col_index % col_half * tiles_col
    local_row = tile_index // tiles_col
    local_col = tile_index % tiles_col
    odd_slots = (
        partner[coarse_nodes:].reshape(coarse_count, tile_size)
        - (jnp.arange(coarse_count, dtype=jnp.int32) * tile_size)[:, None]
    )
    row_table = lax.dynamic_slice_in_dim(odd_slots, row_start, tiles_row, 0)
    col_table = lax.dynamic_slice_in_dim(odd_slots, col_start, tiles_col, 0)
    feature_tiles = features.reshape(tiles_row, tile_size, feat_width)

    def permute_features(tile_block):
        pair_table = pairing_table(row_table, tile_size)
        return jnp.einsum(
            "ijs,ijf->isf", pair_table, tile_block, preferred_element_type=jnp.float32
        ).astype(jnp.bfloat16)

    own_features = lax.cond(row_side == 1, permute_features, keep_block, feature_tiles)
    given_rows = lax.dynamic_slice_in_dim(own_features, (1 - row_side) * half_tile, half_tile, 1)
    kept_rows = lax.dynamic_slice_in_dim(own_features, row_side * half_tile, half_tile, 1)
    partner_features = swapped(given_rows, "row", row_bit)
    merged = (kept_rows.astype(jnp.float32) + partner_features.astype(jnp.float32)).astype(
        jnp.bfloat16
    )
    joined_rows = jnp.dot(
        merged.reshape(tiles_row * half_tile, feat_width),
        join_weight,
        preferred_element_type=jnp.float32,
    )
    extra_table = (pert_slot[:, None] == jnp.arange(slot_count, dtype=jnp.int32)[None, :]).astype(
        jnp.bfloat16
    )
    added_tiles = jnp.einsum(
        "pn,pxy->nxy", extra_table, pert_values, preferred_element_type=jnp.float32
    )
    perturbed = (tile_values.astype(jnp.float32) + added_tiles).astype(jnp.bfloat16)

    def permute_rows(tile_block):
        pair_table = pairing_table(row_table[local_row], tile_size)
        return jnp.einsum(
            "njs,njc->nsc", pair_table, tile_block, preferred_element_type=jnp.float32
        ).astype(jnp.bfloat16)

    def permute_cols(tile_block):
        pair_table = pairing_table(col_table[local_col], tile_size)
        return jnp.einsum(
            "nrj,njs->nrs", tile_block, pair_table, preferred_element_type=jnp.float32
        ).astype(jnp.bfloat16)

    paired = lax.cond(row_side == 1, permute_rows, keep_block, perturbed)
    paired = lax.cond(col_side == 1, permute_cols, keep_block, paired)
    row_given = lax.dynamic_slice_in_dim(paired, (1 - row_side) * half_tile, half_tile, 1)
    row_kept = lax.dynamic_slice_in_dim(paired, row_side * half_tile, half_tile, 1)
    row_partner = swapped(row_given, "row", row_bit)
    row_summed = row_kept.astype(jnp.float32) + row_partner.astype(jnp.float32)
    col_given = lax.dynamic_slice_in_dim(row_summed, (1 - col_side) * half_tile, half_tile, 2)
    col_kept = lax.dynamic_slice_in_dim(row_summed, col_side * half_tile, half_tile, 2)
    col_partner = swapped(col_given, "col", col_bit)
    quarter = col_kept + col_partner
    row_select = (local_row[None, :] == jnp.arange(tiles_row, dtype=jnp.int32)[:, None]).astype(
        jnp.float32
    )
    owned_sums = jnp.dot(
        row_select,
        jnp.sum(quarter, axis=2),
        precision=lax.Precision.HIGHEST,
        preferred_element_type=jnp.float32,
    )
    spread = jnp.zeros((2, row_half, tiles_row, half_tile), jnp.float32)
    spread = lax.dynamic_update_slice(
        spread, owned_sums[None, None], (row_side, row_index % row_half, 0, 0)
    )
    layout = lax.psum(spread, ("row", "col"))
    degree = (
        1.0 + jnp.transpose(layout, (1, 2, 0, 3)).reshape(coarse_count, tile_size) / coarse_nodes
    )
    row_degree = lax.dynamic_slice(
        degree, (row_start, row_side * half_tile), (tiles_row, half_tile)
    )
    col_degree = lax.dynamic_slice(
        degree, (col_start, col_side * half_tile), (tiles_col, half_tile)
    )
    slot_row_degree = row_degree[local_row]
    slot_col_degree = col_degree[local_col]
    normalized = (
        quarter / jnp.sqrt(slot_row_degree[:, :, None] * slot_col_degree[:, None, :])
    ).astype(jnp.bfloat16)
    coarse_features = (
        joined_rows.reshape(tiles_row, half_tile, feat_width) / jnp.sqrt(row_degree)[:, :, None]
    ).astype(jnp.bfloat16)
    coarse_features = coarse_features.reshape(tiles_row * half_tile, feat_width)
    targets = routes[:, 0]
    slot_order = jnp.arange(slot_count, dtype=jnp.int32)
    earlier = jnp.sum(
        (
            (targets[:, None] == targets[None, :]) & (slot_order[None, :] < slot_order[:, None])
        ).astype(jnp.int32),
        axis=1,
    )
    position = targets * capacity + earlier
    place_table = (position[None, :] == jnp.arange(receive_slots, dtype=jnp.int32)[:, None]).astype(
        jnp.bfloat16
    )
    outgoing = jnp.dot(
        place_table,
        normalized.reshape(slot_count, half_tile * half_tile),
        preferred_element_type=jnp.float32,
    ).astype(jnp.bfloat16)
    arrived = lax.all_to_all(
        outgoing.reshape(receive_slots, half_tile, half_tile),
        ("row", "col"),
        split_axis=0,
        concat_axis=0,
        tiled=True,
    )
    return (coarse_features, arrived)


def solution(mesh):
    placed = (
        P("row", None),
        P(),
        P(),
        P(("row", "col")),
        P(("row", "col"), None, None),
        P(("row", "col")),
        P(("row", "col"), None, None),
        P(("row", "col"), None),
    )
    return jax.shard_map(
        local,
        mesh=mesh,
        in_specs=placed,
        out_specs=(P("row", None), P(("row", "col"), None, None)),
        check_vma=False,
    )
```

profile of v0, /device:TPU:32, one launch (start us, length us, event | category | flops | bytes accessed | tf_op | source)
XLA Modules:
  0.0 729.7 jit_solution(8674809250563732469)
XLA Ops:
  7.3 0.9 slice.16
  8.9 17.9 %add_convert_fusion = bf16[104,256,256]{2,0,1:T(8,128)(2,1)} fusion(bf16[104,256,256]{2,1,0:T(8,128)(2,1)} %param.18, bf16[4,256,256]{2,1,0:T(8,128)(2,1)S(1)} %copy-done, s32[4]{0:T(128)} %param.19), kind=kOutput, calls=%fused_computation.22 | convolution fusion | flops 74973600 | bytes 27787280 | tf_op jit(solution)/shard_map/pn,pxy->nxy/dot_general | solution.py:77
  26.9 10.9 %conditional.4 = (bf16[104,256,256]{2,1,0:T(8,128)(2,1)}) conditional(s32[]{:T(128)} %convert_element_type.62, (bf16[104,256,256]{2,0,1:T(8,128)(2,1)}) %tuple.35, (s32[104]{0:T(128)S(1)}, s32[16,256]{1,0:T(8,128)S(1)}, bf16[104,256,256]{2,0,1:T(8,128)(2,1)}) %tuple.29), branch_computations={%region_2.3_spmd, %region_3.4_spmd} | conditional | flops 3503293696 | bytes 27588232 | solution.py:94
  26.9 10.9 %copy.30 = bf16[104,256,256]{2,1,0:T(8,128)(2,1)} copy(bf16[104,256,256]{2,0,1:T(8,128)(2,1)} %get-tuple-element.61) | data formatting | bytes 27262976 | tf_op jit(solution)/shard_map/convert_element_type | solution.py:80
  37.8 18.4 %conditional.5 = (bf16[104,256,256]{1,2,0:T(8,128)(2,1)}) conditional(s32[]{:T(128)} %convert_element_type.66, (bf16[104,256,256]{2,1,0:T(8,128)(2,1)}) %conditional.4, (s32[64,256]{1,0:T(8,128)S(1)}, s32[]{:T(128)}, s32[104]{0:T(128)S(1)}, bf16[104,256,256]{2,1,0:T(8,128)(2,1)}) %tuple.30), branch_computations={%region_4.5_spmd, %region_5.6_spmd} | conditional | flops 3503293696 | bytes 27604620 | solution.py:95
  37.8 18.4 %copy.31 = bf16[104,256,256]{1,2,0:T(8,128)(2,1)} copy(bf16[104,256,256]{2,1,0:T(8,128)(2,1)} %get-tuple-element.63) | data formatting | bytes 27262976 | tf_op jit(solution)/shard_map/cond | solution.py:94
  56.2 6.7 constant_dynamic-slice_fusion.2
  62.9 11.1 %collective-permute-start.1 = (bf16[104,128,256]{1,2,0:T(8,128)(2,1)}, bf16[104,128,256]{1,2,0:T(8,128)(2,1)}, u32[]{:S(2)}, u32[]{:S(2)}) collective-permute-start(bf16[104,128,256]{1,2,0:T(8,128)(2,1)} %constant_dynamic-slice_fusion.2), channel_id=1, source_target_pairs={{0,64},{16,80},{32,96},{48,112},{64,0},{80,16},{96,32},{112,48},{1... | collective-permute-start | bytes 20447240 | tf_op jit(solution)/shard_map/ppermute | solution.py:10
  73.9 147.1 %collective-permute-done.1 = bf16[104,128,256]{1,2,0:T(8,128)(2,1)} collective-permute-done((bf16[104,128,256]{1,2,0:T(8,128)(2,1)}, bf16[104,128,256]{1,2,0:T(8,128)(2,1)}, u32[]{:S(2)}, u32[]{:S(2)}) %collective-permute-start.1) | collective-permute-done | bytes 6815776 | tf_op jit(solution)/shard_map/ppermute | solution.py:10
  221.0 12.7 %convert_add_fusion = f32[104,128,256]{1,2,0:T(8,128)} fusion(bf16[104,128,256]{1,2,0:T(8,128)(2,1)} %collective-permute-done.1, bf16[104,256,256]{1,2,0:T(8,128)(2,1)} %get-tuple-element.80, s32[]{:T(128)S(6)} %select_n.77), kind=kLoop, calls=%fused_computation.24 | loop fusion | flops 10223616 | bytes 27262980 | tf_op jit(solution)/shard_map/add | solution.py:99
  233.7 6.7 constant_dynamic-slice_fusion.1
  240.4 8.8 %collective-permute-start.2 = (f32[104,128,128]{1,2,0:T(8,128)}, f32[104,128,128]{1,2,0:T(8,128)}, u32[]{:S(2)}, u32[]{:S(2)}) collective-permute-start(f32[104,128,128]{1,2,0:T(8,128)} %constant_dynamic-slice_fusion.1), channel_id=1, source_target_pairs={{0,8},{1,9},{2,10},{3,11},{4,12},{5,13},{6,14},{7,15},{8,0},{9,1},... | collective-permute-start | bytes 20447240 | tf_op jit(solution)/shard_map/ppermute | solution.py:10
  249.4 146.3 %collective-permute-done.2 = f32[104,128,128]{1,2,0:T(8,128)} collective-permute-done((f32[104,128,128]{1,2,0:T(8,128)}, f32[104,128,128]{1,2,0:T(8,128)}, u32[]{:S(2)}, u32[]{:S(2)}) %collective-permute-start.2) | collective-permute-done | bytes 6815776 | tf_op jit(solution)/shard_map/ppermute | solution.py:10
  395.7 6.7 fusion.14
  403.2 140.7 %all-reduce.2.cloned.1.call-done = f32[2,4,16,128]{3,2,1,0:T(8,128)} async-done(((f32[2,4,16,128]{3,2,1,0:T(8,128)}), f32[2,4,16,128]{3,2,1,0:T(8,128)}) %all-reduce.2.cloned.1.call-update) | async-done | bytes 65552 | tf_op jit(solution)/shard_map/psum | solution.py:117
  546.1 8.4 %multiply_convert_fusion = bf16[104,128,128]{1,2,0:T(8,128)(2,1)} fusion(f32[104,128]{1,0:T(8,128)S(1)} %gather_fusion.3, f32[104,128]{1,0:T(8,128)S(1)} %gather_fusion.2, f32[104,128,128]{1,2,0:T(8,128)} %collective-permute-done.2, f32[104,128,256]{1,2,0:T(8,128)} %convert_add_fusion, s32[]{:T(128)S(6)} %select_n.84), kind=kLoop, calls=%fused_computation.25 | loop fusion | flops 6815744 | bytes 17145860 | tf_op jit(solution)/shard_map/convert_element_type | solution.py:131
  554.5 5.8 copy.29
  560.3 8.3 %fusion.11 = bf16[32,8,128,128]{3,1,2,0:T(8,128)(2,1)} fusion(bf16[13,8,128,128]{3,2,1,0:T(8,128)(2,1)} %bitcast.36, s32[104]{0:T(128)S(1)} %multiply_add_fusion), kind=kOutput, calls=%fused_computation.27 | convolution fusion | flops 876636160 | bytes 11796896 | tf_op jit(solution)/shard_map/dot_general | solution.py:148
  568.7 9.2 %copy.34 = bf16[32,8,128,128]{3,2,1,0:T(8,128)(2,1)} copy(bf16[32,8,128,128]{3,1,2,0:T(8,128)(2,1)} %fusion.11) | data formatting | bytes 16777216
  577.9 6.9 all-to-all-start
  584.9 4.1 collective-permute-start
  589.0 121.7 %collective-permute-done = bf16[16,128,256]{2,1,0:T(8,128)(2,1)S(1)} collective-permute-done((bf16[16,128,256]{2,1,0:T(8,128)(2,1)S(1)}, bf16[16,128,256]{2,1,0:T(8,128)(2,1)S(1)}, u32[]{:S(2)}, u32[]{:S(2)}) %collective-permute-start) | collective-permute-done | bytes 1048608 | tf_op jit(solution)/shard_map/ppermute | solution.py:10
  710.7 1.5 divide_convert_fusion
  712.2 10.6 %copy.61 = bf16[256,128,128]{2,1,0:T(8,128)(2,1)} copy(bf16[256,128,128]{2,1,0:T(8,128)(2,1)} %all-to-all-done) | data formatting | bytes 16777216
  (35 shorter events, 4.1 us)
Async XLA Ops:
  7.2 1.7 copy-start
  7.2 536.8 %all-reduce.2.cloned.1.call-start = ((), (), s32[]{:S(2)}) async-start(), calls=%async_computation.1 | async-start | bytes 131072 | tf_op jit(solution)/shard_map/psum | solution.py:117
  62.9 158.1 %collective-permute-start.1 = (bf16[104,128,256]{1,2,0:T(8,128)(2,1)}, bf16[104,128,256]{1,2,0:T(8,128)(2,1)}, u32[]{:S(2)}, u32[]{:S(2)}) collective-permute-start(bf16[104,128,256]{1,2,0:T(8,128)(2,1)} %constant_dynamic-slice_fusion.2), channel_id=1, source_target_pairs={{0,64},{16,80},{32,96},{48,112},{64,0},{80,16},{96,32},{112,48},{1... | collective-permute-start | bytes 20447240 | tf_op jit(solution)/shard_map/ppermute | solution.py:10
  233.7 15.5 %copy-start.5 = (s32[104,2]{0,1:T(2,128)S(1)}, s32[104,2]{0,1:T(2,128)}, u32[]{:S(2)}) copy-start(s32[104,2]{0,1:T(2,128)} %param.21) | copy-start | bytes 2500
  240.4 155.3 %collective-permute-start.2 = (f32[104,128,128]{1,2,0:T(8,128)}, f32[104,128,128]{1,2,0:T(8,128)}, u32[]{:S(2)}, u32[]{:S(2)}) collective-permute-start(f32[104,128,128]{1,2,0:T(8,128)} %constant_dynamic-slice_fusion.1), channel_id=1, source_target_pairs={{0,8},{1,9},{2,10},{3,11},{4,12},{5,13},{6,14},{7,15},{8,0},{9,1},... | collective-permute-start | bytes 20447240 | tf_op jit(solution)/shard_map/ppermute | solution.py:10
  402.5 0.6 copy-start.3
  577.9 6.9 copy-start.2
  577.9 134.3 %all-to-all-start = ((bf16[256,128,128]{2,1,0:T(8,128)(2,1)}), bf16[256,128,128]{2,1,0:T(8,128)(2,1)}, u32[]{:S(2)}, u32[]{:S(2)}) async-start(bf16[256,128,128]{2,1,0:T(8,128)(2,1)} %bitcast.35), calls=%async_computation | async-start | bytes 16777216 | tf_op jit(solution)/shard_map/all_to_all | solution.py:153
  584.8 125.9 %copy-start.4 = (bf16[256,256]{1,0:T(8,128)(2,1)S(1)}, bf16[256,256]{1,0:T(8,128)(2,1)}, u32[]{:S(2)}) copy-start(bf16[256,256]{1,0:T(8,128)(2,1)} %param.15) | copy-start | bytes 393220
  584.9 125.8 %collective-permute-start = (bf16[16,128,256]{2,1,0:T(8,128)(2,1)S(1)}, bf16[16,128,256]{2,1,0:T(8,128)(2,1)S(1)}, u32[]{:S(2)}, u32[]{:S(2)}) collective-permute-start(bf16[16,128,256]{2,1,0:T(8,128)(2,1)S(1)} %constant_dynamic-slice_fusion.3), channel_id=1, source_target_pairs={{0,64},{16,80},{32,96},{48,112},{64,0},{80,16},{96,32},{112,48},{1... | collective-permute-start | bytes 3145736 | tf_op jit(solution)/shard_map/ppermute | solution.py:10
  712.2 10.6 %copy-start.1 = (bf16[4,256,256]{2,1,0:T(8,128)(2,1)S(1)}, bf16[4,256,256]{2,1,0:T(8,128)(2,1)}, u32[]{:S(2)}) copy-start(bf16[4,256,256]{2,1,0:T(8,128)(2,1)} %param.20) | copy-start | bytes 1572868
Sparse Core Ops, SparseCore 0:
  403.3 140.5 all-reduce.1
where the time goes:
time: 731 us; the launch traced here: 730 us
  waiting for transfers between devices  556 us (76%)
  local copies, waits for them, and re-layouts  71.3 us (10%)
  starting transfers between devices  30.9 us (4%)
  other arithmetic  29.6 us (4%)
  matrix products  27.9 us (4%)
  between operations  14.2 us (2%)
    ppermute x3, waiting for transfers between devices, swapped(): return lax.ppermute(value, axis, pairs)  415 us
    psum x1, waiting for transfers between devices, local(): layout = lax.psum(spread, ('row', 'col'))  141 us
    ppermute x3, starting transfers between devices, swapped(): return lax.ppermute(value, axis, pairs)  23.9 us
    unnamed x15, local copies, waits for them, and re-layouts  20.5 us
    cond x1, local copies, waits for them, and re-layouts, local(): paired = lax.cond(row_side == 1, permute_rows, keep_block, perturbed)  18.4 us
    dot_general x1, matrix products, local(): jnp.einsum('pn,pxy->nxy', extra_table, pert_values, preferred_element_typ...  17.9 us
  transfers between devices with their start and end apart: 5, of which 4 were waited for; matrix products, arithmetic and copies ran while one was open for 0% of the time, Pallas kernels for 0%

commit v1 on v0

--- a/solution.py
+++ b/solution.py
@@ -114,7 +114,7 @@
     spread = lax.dynamic_update_slice(
         spread, owned_sums[None, None], (row_side, row_index % row_half, 0, 0)
     )
-    layout = lax.psum(spread, ("row", "col"))
+    layout = jnp.sum(lax.all_gather(spread, ("row", "col")), axis=0)
     degree = (
         1.0 + jnp.transpose(layout, (1, 2, 0, 3)).reshape(coarse_count, tile_size) / coarse_nodes
     )

time: 731 us -> 664 us (0.908)
  waiting for transfers between devices: 556 us -> 485 us
    psum x1 -> x0, waiting for transfers between devices: 141 us -> none  [local(): layout = lax.psum(spread, ('row', 'col'))]
    all_gather x0 -> x1, waiting for transfers between devices: none -> 70.4 us  [local(): layout = jnp.sum(lax.all_gather(spread, ('row', 'col')), axis=0)]
where the time goes in v1:
time: 664 us; the launch traced here: 663 us
  waiting for transfers between devices  485 us (73%)
  local copies, waits for them, and re-layouts  71.3 us (11%)
  other arithmetic  32.6 us (5%)
  starting transfers between devices  31.9 us (5%)
  matrix products  27.9 us (4%)
  between operations  14.2 us (2%)
    ppermute x3, waiting for transfers between devices, swapped(): return lax.ppermute(value, axis, pairs)  415 us
    all_gather x1, waiting for transfers between devices, local(): layout = jnp.sum(lax.all_gather(spread, ('row', 'col')), axis=0)  70.4 us
    ppermute x3, starting transfers between devices, swapped(): return lax.ppermute(value, axis, pairs)  24.2 us
    unnamed x15, local copies, waits for them, and re-layouts  20.5 us
    cond x1, local copies, waits for them, and re-layouts, local(): paired = lax.cond(row_side == 1, permute_rows, keep_block, perturbed)  18.4 us
    dot_general x1, matrix products, local(): jnp.einsum('pn,pxy->nxy', extra_table, pert_values, preferred_element_typ...  17.9 us
  transfers between devices with their start and end apart: 5, of which 4 were waited for; matrix products, arithmetic and copies ran while one was open for 0% of the time, Pallas kernels for 0%

profile of v1, /device:TPU:32, one launch (start us, length us, event | category | flops | bytes accessed | tf_op | source)
XLA Modules:
  0.0 663.3 jit_solution(11039430712430083147)
XLA Ops:
  8.9 17.9 %add_convert_fusion = bf16[104,256,256]{2,0,1:T(8,128)(2,1)} fusion(bf16[104,256,256]{2,1,0:T(8,128)(2,1)} %param.18, bf16[4,256,256]{2,1,0:T(8,128)(2,1)S(1)} %copy-done, s32[4]{0:T(128)} %param.19), kind=kOutput, calls=%fused_computation.22 | convolution fusion | flops 74973600 | bytes 27787280 | tf_op jit(solution)/shard_map/pn,pxy->nxy/dot_general | solution.py:77
  26.9 10.9 %conditional.4 = (bf16[104,256,256]{2,1,0:T(8,128)(2,1)}) conditional(s32[]{:T(128)} %convert_element_type.62, (bf16[104,256,256]{2,0,1:T(8,128)(2,1)}) %tuple.36, (s32[104]{0:T(128)S(1)}, s32[16,256]{1,0:T(8,128)S(1)}, bf16[104,256,256]{2,0,1:T(8,128)(2,1)}) %tuple.29), branch_computations={%region_2.3_spmd, %region_3.4_spmd} | conditional | flops 3503293696 | bytes 27588232 | solution.py:94
  26.9 10.9 %copy.35 = bf16[104,256,256]{2,1,0:T(8,128)(2,1)} copy(bf16[104,256,256]{2,0,1:T(8,128)(2,1)} %get-tuple-element.64) | data formatting | bytes 27262976 | tf_op jit(solution)/shard_map/convert_element_type | solution.py:80
  37.8 18.4 %conditional.5 = (bf16[104,256,256]{1,2,0:T(8,128)(2,1)}) conditional(s32[]{:T(128)} %convert_element_type.66, (bf16[104,256,256]{2,1,0:T(8,128)(2,1)}) %conditional.4, (s32[64,256]{1,0:T(8,128)S(1)}, s32[]{:T(128)}, s32[104]{0:T(128)S(1)}, bf16[104,256,256]{2,1,0:T(8,128)(2,1)}) %tuple.30), branch_computations={%region_4.5_spmd, %region_5.6_spmd} | conditional | flops 3503293696 | bytes 27604620 | solution.py:95
  37.8 18.4 %copy.36 = bf16[104,256,256]{1,2,0:T(8,128)(2,1)} copy(bf16[104,256,256]{2,1,0:T(8,128)(2,1)} %get-tuple-element.66) | data formatting | bytes 27262976 | tf_op jit(solution)/shard_map/cond | solution.py:94
  56.2 6.7 %constant_dynamic-slice_fusion.2 = bf16[104,128,256]{1,2,0:T(8,128)(2,1)} fusion(bf16[104,256,256]{1,2,0:T(8,128)(2,1)} %get-tuple-element.83, s32[]{:T(128)S(6)} %select_n.78), kind=kLoop, calls=%fused_computation.54 | loop fusion | bytes 13631492 | tf_op jit(solution)/shard_map/dynamic_slice | solution.py:96
  62.9 11.1 %collective-permute-start.1 = (bf16[104,128,256]{1,2,0:T(8,128)(2,1)}, bf16[104,128,256]{1,2,0:T(8,128)(2,1)}, u32[]{:S(2)}, u32[]{:S(2)}) collective-permute-start(bf16[104,128,256]{1,2,0:T(8,128)(2,1)} %constant_dynamic-slice_fusion.2), channel_id=1, source_target_pairs={{0,64},{16,80},{32,96},{48,112},{64,0},{80,16},{96,32},{112,48},{1... | collective-permute-start | bytes 20447240 | tf_op jit(solution)/shard_map/ppermute | solution.py:10
  73.9 147.1 %collective-permute-done.1 = bf16[104,128,256]{1,2,0:T(8,128)(2,1)} collective-permute-done((bf16[104,128,256]{1,2,0:T(8,128)(2,1)}, bf16[104,128,256]{1,2,0:T(8,128)(2,1)}, u32[]{:S(2)}, u32[]{:S(2)}) %collective-permute-start.1) | collective-permute-done | bytes 6815776 | tf_op jit(solution)/shard_map/ppermute | solution.py:10
  221.0 12.7 %convert_add_fusion = f32[104,128,256]{1,2,0:T(8,128)} fusion(bf16[104,128,256]{1,2,0:T(8,128)(2,1)} %collective-permute-done.1, bf16[104,256,256]{1,2,0:T(8,128)(2,1)} %get-tuple-element.83, s32[]{:T(128)S(6)} %select_n.77), kind=kLoop, calls=%fused_computation.24 | loop fusion | flops 10223616 | bytes 27262980 | tf_op jit(solution)/shard_map/add | solution.py:99
  233.7 6.7 %constant_dynamic-slice_fusion.1 = f32[104,128,128]{1,2,0:T(8,128)} fusion(f32[104,128,256]{1,2,0:T(8,128)} %convert_add_fusion, s32[]{:T(128)S(6)} %select_n.85), kind=kLoop, calls=%fused_computation.53 | loop fusion | bytes 13631492 | tf_op jit(solution)/shard_map/dynamic_slice | solution.py:100
  240.4 8.8 %collective-permute-start.2 = (f32[104,128,128]{1,2,0:T(8,128)}, f32[104,128,128]{1,2,0:T(8,128)}, u32[]{:S(2)}, u32[]{:S(2)}) collective-permute-start(f32[104,128,128]{1,2,0:T(8,128)} %constant_dynamic-slice_fusion.1), channel_id=1, source_target_pairs={{0,8},{1,9},{2,10},{3,11},{4,12},{5,13},{6,14},{7,15},{8,0},{9,1},... | collective-permute-start | bytes 20447240 | tf_op jit(solution)/shard_map/ppermute | solution.py:10
  249.2 146.5 %collective-permute-done.2 = f32[104,128,128]{1,2,0:T(8,128)} collective-permute-done((f32[104,128,128]{1,2,0:T(8,128)}, f32[104,128,128]{1,2,0:T(8,128)}, u32[]{:S(2)}, u32[]{:S(2)}) %collective-permute-start.2) | collective-permute-done | bytes 6815776 | tf_op jit(solution)/shard_map/ppermute | solution.py:10
  395.7 6.7 %fusion.14 = f32[104,128]{1,0:T(8,128)S(1)} fusion(f32[104,128,128]{1,2,0:T(8,128)} %collective-permute-done.2, f32[104,128,256]{1,2,0:T(8,128)} %convert_add_fusion, s32[]{:T(128)S(6)} %select_n.84), kind=kLoop, calls=%fused_computation.30 | loop fusion | flops 3394560 | bytes 13684740 | tf_op jit(solution)/shard_map/reduce_sum | solution.py:109
  403.4 70.4 %all-gather.2.cloned.1.call-done = f32[128,2,4,16,128]{4,3,2,1,0:T(8,128)} async-done(((f32[1,2,4,16,128]{4,3,2,1,0:T(8,128)}), f32[128,2,4,16,128]{4,3,2,1,0:T(8,128)}) %all-gather.2.cloned.1.call-update) | async-done | bytes 8388624 | tf_op jit(solution)/shard_map/all_gather | solution.py:117
  473.8 3.9 reduce_sum.28
  479.0 8.4 %multiply_convert_fusion = bf16[104,128,128]{1,2,0:T(8,128)(2,1)} fusion(f32[104,128]{1,0:T(8,128)S(1)} %gather_fusion.3, f32[104,128]{1,0:T(8,128)S(1)} %gather_fusion.2, f32[104,128,128]{1,2,0:T(8,128)} %collective-permute-done.2, f32[104,128,256]{1,2,0:T(8,128)} %convert_add_fusion, s32[]{:T(128)S(6)} %select_n.84), kind=kLoop, calls=%fused_computation.25 | loop fusion | flops 6815744 | bytes 17145860 | tf_op jit(solution)/shard_map/convert_element_type | solution.py:131
  487.4 5.8 copy.34
  493.2 8.3 %fusion.11 = bf16[32,8,128,128]{3,1,2,0:T(8,128)(2,1)} fusion(bf16[13,8,128,128]{3,2,1,0:T(8,128)(2,1)} %bitcast.36, s32[104]{0:T(128)S(1)} %multiply_add_fusion), kind=kOutput, calls=%fused_computation.27 | convolution fusion | flops 876636160 | bytes 11796896 | tf_op jit(solution)/shard_map/dot_general | solution.py:148
  501.6 9.2 %copy.39 = bf16[32,8,128,128]{3,2,1,0:T(8,128)(2,1)} copy(bf16[32,8,128,128]{3,1,2,0:T(8,128)(2,1)} %fusion.11) | data formatting | bytes 16777216
  510.8 7.7 %all-to-all-start = ((bf16[256,128,128]{2,1,0:T(8,128)(2,1)}), bf16[256,128,128]{2,1,0:T(8,128)(2,1)}, u32[]{:S(2)}, u32[]{:S(2)}) async-start(bf16[256,128,128]{2,1,0:T(8,128)(2,1)} %bitcast.35), calls=%async_computation | async-start | bytes 16777216 | tf_op jit(solution)/shard_map/all_to_all | solution.py:153
  518.6 4.3 collective-permute-start
  522.9 121.5 %collective-permute-done = bf16[16,128,256]{2,1,0:T(8,128)(2,1)S(1)} collective-permute-done((bf16[16,128,256]{2,1,0:T(8,128)(2,1)S(1)}, bf16[16,128,256]{2,1,0:T(8,128)(2,1)S(1)}, u32[]{:S(2)}, u32[]{:S(2)}) %collective-permute-start) | collective-permute-done | bytes 1048608 | tf_op jit(solution)/shard_map/ppermute | solution.py:10
  644.4 1.5 divide_convert_fusion
  645.8 10.6 %copy.65 = bf16[256,128,128]{2,1,0:T(8,128)(2,1)} copy(bf16[256,128,128]{2,1,0:T(8,128)(2,1)} %all-to-all-done) | data formatting | bytes 16777216
  (36 shorter events, 4.2 us)
Async XLA Ops:
  7.2 1.7 copy-start
  7.2 466.6 %all-gather.2.cloned.1.call-start = ((), (), s32[]{:S(2)}) async-start(), calls=%async_computation.1 | async-start | bytes 8454144 | tf_op jit(solution)/shard_map/all_gather | solution.py:117
  62.9 158.1 %collective-permute-start.1 = (bf16[104,128,256]{1,2,0:T(8,128)(2,1)}, bf16[104,128,256]{1,2,0:T(8,128)(2,1)}, u32[]{:S(2)}, u32[]{:S(2)}) collective-permute-start(bf16[104,128,256]{1,2,0:T(8,128)(2,1)} %constant_dynamic-slice_fusion.2), channel_id=1, source_target_pairs={{0,64},{16,80},{32,96},{48,112},{64,0},{80,16},{96,32},{112,48},{1... | collective-permute-start | bytes 20447240 | tf_op jit(solution)/shard_map/ppermute | solution.py:10
  240.4 155.3 %collective-permute-start.2 = (f32[104,128,128]{1,2,0:T(8,128)}, f32[104,128,128]{1,2,0:T(8,128)}, u32[]{:S(2)}, u32[]{:S(2)}) collective-permute-start(f32[104,128,128]{1,2,0:T(8,128)} %constant_dynamic-slice_fusion.1), channel_id=1, source_target_pairs={{0,8},{1,9},{2,10},{3,11},{4,12},{5,13},{6,14},{7,15},{8,0},{9,1},... | collective-permute-start | bytes 20447240 | tf_op jit(solution)/shard_map/ppermute | solution.py:10
  249.2 154.0 %copy-start.5 = (s32[104,2]{0,1:T(2,128)S(1)}, s32[104,2]{0,1:T(2,128)}, u32[]{:S(2)}) copy-start(s32[104,2]{0,1:T(2,128)} %param.21) | copy-start | bytes 2500
  402.5 0.6 copy-start.3
  510.8 7.7 %copy-start.2 = (bf16[4096,256]{1,0:T(8,128)(2,1)S(1)}, bf16[4096,256]{1,0:T(8,128)(2,1)}, u32[]{:S(2)}) copy-start(bf16[4096,256]{1,0:T(8,128)(2,1)} %param.14) | copy-start | bytes 6291460
  510.8 135.1 %all-to-all-start = ((bf16[256,128,128]{2,1,0:T(8,128)(2,1)}), bf16[256,128,128]{2,1,0:T(8,128)(2,1)}, u32[]{:S(2)}, u32[]{:S(2)}) async-start(bf16[256,128,128]{2,1,0:T(8,128)(2,1)} %bitcast.35), calls=%async_computation | async-start | bytes 16777216 | tf_op jit(solution)/shard_map/all_to_all | solution.py:153
  518.4 125.9 %copy-start.4 = (bf16[256,256]{1,0:T(8,128)(2,1)S(1)}, bf16[256,256]{1,0:T(8,128)(2,1)}, u32[]{:S(2)}) copy-start(bf16[256,256]{1,0:T(8,128)(2,1)} %param.15) | copy-start | bytes 393220
  518.6 125.8 %collective-permute-start = (bf16[16,128,256]{2,1,0:T(8,128)(2,1)S(1)}, bf16[16,128,256]{2,1,0:T(8,128)(2,1)S(1)}, u32[]{:S(2)}, u32[]{:S(2)}) collective-permute-start(bf16[16,128,256]{2,1,0:T(8,128)(2,1)S(1)} %constant_dynamic-slice_fusion.3), channel_id=1, source_target_pairs={{0,64},{16,80},{32,96},{48,112},{64,0},{80,16},{96,32},{112,48},{1... | collective-permute-start | bytes 3145736 | tf_op jit(solution)/shard_map/ppermute | solution.py:10
  645.8 10.6 %copy-start.1 = (bf16[4,256,256]{2,1,0:T(8,128)(2,1)S(1)}, bf16[4,256,256]{2,1,0:T(8,128)(2,1)}, u32[]{:S(2)}) copy-start(bf16[4,256,256]{2,1,0:T(8,128)(2,1)} %param.20) | copy-start | bytes 1572868
Sparse Core Ops, SparseCore 0:
  403.3 70.4 all-gather.1
